TPU v7x, 32 devices: a whole 2x2x4 slice. The times are simulated.
32 devices in a mesh: gx: 16 (over z, y, x), gy: 2 (over core).
Axes of the slice: x: 2, y: 2, z: 4, core: 2. Of those that a mesh axis runs over, the one named last changes fastest.
Arguments:
- snapshot: bfloat16 [3, 128, 32, 1024], P(None, 'gx', 'gy'), may hold values from -6 to 6
- basis: bfloat16 [3, 16, 4, 128, 512], P(None, 'gx', 'gy'), may hold values from -3000 to 3000
- taps: bfloat16 [3, 17], replicated, may hold values from 0.099609375 to 1
Outputs:
- new_modes: bfloat16 [3, 16, 4, 128, 512], P(None, 'gx', 'gy')
- new_mode: float32 [3, 16, 4, 128], P(None, 'gx', 'gy')
- factor: float32 [513, 513], replicated
All inputs are finite; a program needn't handle non-finite values.
Results may differ from a plain program's by a relative error of at most 0.0012.
The roundings to bfloat16 on the way count: a program that leaves them out, or rounds other values in their place, can miss the bound.
Values sent between devices are 32-bit elements; how exact they have to be, the bound alone decides.
No kernel may reach another device: no remote copies, remote signals or barrier semaphores. Data moves between devices by JAX's collectives and lax.ppermute only.
A program may use at most 64 MiB of HBM per device.

v0:
```python
import jax
import jax.numpy as jnp
from jax import lax
from jax.sharding import PartitionSpec as P

STRIDE = 8


def padded(block, sides, width, periodic):
    for axis, dim in sides:
        count = lax.axis_size(axis)
        forward = [(i, i + 1) for i in range(count - 1)]
        if periodic:
            forward.append((count - 1, 0))
        backward = [(target, source) for source, target in forward]
        low = lax.ppermute(
            lax.slice_in_dim(block, block.shape[dim] - width, None, axis=dim), axis, forward
        )
        high = lax.ppermute(lax.slice_in_dim(block, 0, width, axis=dim), axis, backward)
        block = jnp.concatenate([low, block, high], axis=dim)
    return block


def band(taps_row, length, out_len, shift, wrap):
    rows = jnp.arange(length, dtype=jnp.int32)[:, None]
    cols = jnp.arange(out_len, dtype=jnp.int32)[None, :]
    lag = rows - STRIDE * cols + shift
    if wrap:
        lag = lag % length
    hits = lag[:, :, None] == jnp.arange(2 * STRIDE + 1, dtype=jnp.int32)[None, None, :]
    return jnp.sum(jnp.where(hits, taps_row[None, None, :], jnp.zeros((), taps_row.dtype)), axis=-1)


def local(snapshot, basis, taps):
    comps, cells_x, cells_y, cells_z = snapshot.shape
    modes = basis.shape[-1]
    flat_rows = basis.reshape(-1, modes)
    total = flat_rows.shape[0] * lax.axis_size("gx") * lax.axis_size("gy")
    mode_part = lax.psum(
        jnp.einsum("rk,rj->kj", flat_rows, flat_rows, preferred_element_type=jnp.float32),
        ("gx", "gy"),
    )
    matrix_z = band(taps[2], cells_z, cells_z // STRIDE, STRIDE, True)
    along_z = jnp.dot(snapshot.reshape(-1, cells_z), matrix_z, preferred_element_type=jnp.float32)
    along_z = along_z.reshape(comps, cells_x, cells_y, cells_z // STRIDE)
    padded_y = padded(along_z, (("gy", 2),), STRIDE, False)
    matrix_y = band(taps[1], cells_y + 2 * STRIDE, cells_y // STRIDE, 0, False).astype(jnp.float32)
    along_y = jnp.einsum("cxyz,yf->cxfz", padded_y, matrix_y, precision=lax.Precision.HIGHEST)
    padded_x = padded(along_y, (("gx", 1),), STRIDE, True)
    matrix_x = band(taps[0], cells_x + 2 * STRIDE, cells_x // STRIDE, 0, False).astype(jnp.float32)
    along_x = jnp.einsum("cxyz,xf->cfyz", padded_x, matrix_x, precision=lax.Precision.HIGHEST)
    filtered = along_x.astype(jnp.bfloat16).reshape(-1)
    stack = jnp.concatenate([flat_rows, filtered[:, None]], axis=1)
    fresh_wide = filtered.astype(jnp.float32)
    cross, square = lax.psum(
        (
            jnp.einsum("rk,r->k", flat_rows, filtered, preferred_element_type=jnp.float32),
            jnp.sum(fresh_wide * fresh_wide),
        ),
        ("gx", "gy"),
    )
    upper_rows = jnp.concatenate([mode_part, cross[:, None]], axis=1)
    last_row = jnp.concatenate([cross, square[None]])[None, :]
    gram = jnp.concatenate([upper_rows, last_row], axis=0)
    gram = gram / total
    lower = jnp.linalg.cholesky(gram)
    solved = lax.linalg.triangular_solve(
        lower, stack.astype(jnp.float32), left_side=False, lower=True, transpose_a=True
    )
    new_modes = solved[:, :modes].astype(jnp.bfloat16).reshape(basis.shape)
    new_mode = solved[:, modes].reshape(basis.shape[:-1])
    return (new_modes, new_mode, lower.T)


def solution(mesh):
    in_specs = (P(None, "gx", "gy", None), P(None, "gx", "gy", None, None), P())
    out_specs = (P(None, "gx", "gy", None, None), P(None, "gx", "gy", None), P())
    return jax.shard_map(local, mesh=mesh, in_specs=in_specs, out_specs=out_specs, check_vma=False)
```

profile of v0, /device:TPU:0, one launch (start us, length us, event | category | flops | bytes accessed | tf_op | source)
XLA Modules:
  0.0 347.1 jit_solution(4015166581742099439)
XLA Ops:
  7.2 0.8 slice_bitcast_fusion.14
  8.3 0.9 fusion.1
  9.2 0.4 convolution_bitcast_fusion.1
  9.8 2.4 collective-permute-start
  12.2 1.3 collective-permute-start.1
  13.5 1.6 convolution_bitcast_fusion
  15.7 2.4 collective-permute-start.2
  18.1 4.1 %collective-permute-start.3 = (f32[3,8,2,128]{3,2,1,0:T(2,128)S(1)}, f32[3,8,2,128]{3,2,1,0:T(2,128)S(1)}, u32[]{:S(2)}, u32[]{:S(2)}) collective-permute-start(f32[3,8,2,128]{3,2,1,0:T(2,128)S(1)} %convolution_bitcast_fusion.2), channel_id=1, source_target_pairs={{2,0},{4,2},{6,4},{8,6},{10,8},{12,10},{14,12},{16,14},{18,16},{20... | collective-permute-start | bytes 73736 | tf_op jit(solution)/shard_map/ppermute | solution.py:19
  22.2 1.7 collective-permute-done.2
  24.1 0.6 multiply_reduce_fusion
  24.9 41.3 %all-reduce.3 = (f32[1]{0:T(128)}, f32[512]{0:T(512)S(1)}) all-reduce(f32[1]{0:T(128)} %bitcast.19, f32[512]{0:T(512)S(1)} %bitcast.151), channel_id=1, replica_groups=mesh['gx'=16,'gy'=2] {'gx','gy'}, use_global_device_ids=true, to_apply=%region_6.7 | all-reduce | flops 513 | bytes 4104 | tf_op jit(solution)/shard_map/psum | solution.py:55
  66.5 0.7 pad_maximum_fusion.4
  67.3 81.6 %all-reduce.6.cloned.1.call-done = f32[512,512]{0,1:T(8,128)} async-done(((f32[512,512]{0,1:T(8,128)}), f32[512,512]{0,1:T(8,128)}) %all-reduce.6.cloned.1.call-update) | async-done | bytes 1048592 | tf_op jit(solution)/shard_map/psum | solution.py:39
  148.9 2.4 maximum_multiply_fusion
  151.3 1.8 copy.62
  153.1 1.5 fusion.10
  154.6 1.0 copy-done.4
  155.6 0.5 cholesky.348
  156.1 11.7 %cholesky.131 = f32[128,128]{1,0:T(8,128)S(1)} custom-call(f32[128,128]{1,0:T(8,128)S(1)} %cholesky.333), custom_call_target="Cholesky" | custom-call | tf_op jit(solution)/shard_map/jit(cholesky)/cholesky | solution.py:66
  168.0 9.8 %custom-call.35 = f32[1,128,128]{1,2,0:T(8,128)S(1)} custom-call(f32[1,128,128]{2,1,0:T(8,128)S(1)} %get-tuple-element.51), custom_call_target="InvertDiagBlocksLowerTriangular" | custom-call | tf_op jit(solution)/shard_map/jit(cholesky)/cholesky | solution.py:66
  177.8 1.4 constant_dynamic-update-slice_fusion.2
  179.2 1.4 convolution_subtract_fusion.3
  180.6 11.7 %cholesky.264 = f32[128,128]{1,0:T(8,128)S(1)} custom-call(f32[128,128]{1,0:T(8,128)S(1)} %cholesky.337), custom_call_target="Cholesky" | custom-call | tf_op jit(solution)/shard_map/jit(cholesky)/cholesky | solution.py:66
  192.4 9.9 %custom-call.36 = f32[1,128,128]{1,2,0:T(8,128)S(1)} custom-call(f32[1,128,128]{2,1,0:T(8,128)S(1)} %get-tuple-element.48), custom_call_target="InvertDiagBlocksLowerTriangular" | custom-call | tf_op jit(solution)/shard_map/jit(cholesky)/cholesky | solution.py:66
  202.3 0.4 convolution_dynamic-update-slice_fusion
  202.7 1.3 convolution_subtract_fusion.4
  204.0 11.7 %cholesky.285 = f32[128,128]{1,0:T(8,128)S(1)} custom-call(f32[128,128]{1,0:T(8,128)S(1)} %cholesky.342), custom_call_target="Cholesky" | custom-call | tf_op jit(solution)/shard_map/jit(cholesky)/cholesky | solution.py:66
  215.8 9.8 %custom-call.37 = f32[1,128,128]{1,2,0:T(8,128)S(1)} custom-call(f32[1,128,128]{2,1,0:T(8,128)S(1)} %get-tuple-element.45), custom_call_target="InvertDiagBlocksLowerTriangular" | custom-call | tf_op jit(solution)/shard_map/jit(cholesky)/cholesky | solution.py:66
  225.8 1.3 convolution_subtract_fusion.5
  227.1 11.9 %cholesky.304 = f32[128,128]{1,0:T(8,128)S(1)} custom-call(f32[128,128]{1,0:T(8,128)S(1)} %cholesky.347), custom_call_target="Cholesky" | custom-call | tf_op jit(solution)/shard_map/jit(cholesky)/cholesky | solution.py:66
  239.1 9.8 %custom-call.38 = f32[1,128,128]{1,2,0:T(8,128)S(1)} custom-call(f32[1,128,128]{2,1,0:T(8,128)S(1)} %get-tuple-element.42), custom_call_target="InvertDiagBlocksLowerTriangular" | custom-call | tf_op jit(solution)/shard_map/jit(cholesky)/cholesky | solution.py:66
  249.2 0.6 multiply_reduce_fusion.1
  251.2 0.7 compare_reduce_fusion.1
  252.0 0.6 compare_reduce_fusion
  252.6 0.6 compare_reduce_fusion.2
  255.8 1.2 fusion.20
  257.0 0.5 triangular_solve.195
  257.6 0.5 copy-done.3
  258.1 11.3 %while.1 = (s32[]{:T(128)}, f32[513,513]{1,0:T(8,128)}, s32[4,2]{0,1:T(2,128)S(1)}, f32[4,128,128]{2,1,0:T(8,128)S(1)}, s32[]{:T(128)}) while((s32[]{:T(128)}, f32[513,513]{1,0:T(8,128)}, s32[4,2]{0,1:T(2,128)S(1)}, f32[4,128,128]{2,1,0:T(8,128)S(1)}, s32[]{:T(128)}) %tuple.51), condition=%wide.while_cond, body=%wide.while_body.sunk | while | flops 2 | bytes 131181 | solution.py:67
  258.2 0.5 fusion.83
  258.7 2.2 bitcast_dynamic-update-slice_fusion.2
  261.0 0.5 fusion.83
  261.5 2.2 bitcast_dynamic-update-slice_fusion.2
  263.8 0.5 fusion.83
  264.4 2.2 bitcast_dynamic-update-slice_fusion.2
  266.7 0.5 fusion.83
  267.2 2.2 bitcast_dynamic-update-slice_fusion.2
  269.4 0.7 fusion.53
  270.2 49.1 %custom-call.39 = f32[5,128,128]{1,2,0:T(8,128)S(1)} custom-call(f32[5,128,128]{2,1,0:T(8,128)S(1)} %pad_maximum_fusion.1), custom_call_target="InvertDiagBlocksLowerTriangular" | custom-call | tf_op jit(solution)/shard_map/triangular_solve | solution.py:67
  319.4 0.6 triangular_solve.205
  319.9 1.1 bitcast_convert_fusion
  321.0 1.6 convolution_subtract_fusion.1
  322.6 0.5 fusion.74
  323.3 2.3 convolution_subtract_fusion.2
  325.6 1.1 fusion.73
  326.9 3.0 convolution_subtract_fusion
  329.9 2.0 fusion.72
  331.9 0.9 copy.73
  332.8 1.9 fusion.17
  334.7 1.0 fusion.34
  335.8 0.6 triangular_solve.193
  336.4 1.1 copy.88
  337.5 1.5 copy.76
  339.0 1.0 pad_maximum_fusion
  (61 shorter events, 3.5 us)
Async XLA Ops:
  7.2 2.1 copy-start
  7.2 141.7 %all-reduce.6.cloned.1.call-start = ((), (), s32[]{:S(2)}) async-start(), calls=%async_computation | async-start | bytes 2097152 | tf_op jit(solution)/shard_map/psum | solution.py:39
  8.3 5.2 %copy-start.1 = (bf16[3,1,2,128,512]{4,3,2,1,0:T(8,128)(2,1)S(1)}, bf16[3,1,2,128,512]{4,3,2,1,0:T(8,128)(2,1)}, u32[]{:S(2)}) copy-start(bf16[3,1,2,128,512]{4,3,2,1,0:T(8,128)(2,1)} %param.4) | copy-start | bytes 2359300
  9.8 5.7 %collective-permute-start = (f32[3,8,8,128]{3,2,1,0:T(8,128)S(1)}, f32[3,8,8,128]{3,2,1,0:T(8,128)S(1)}, u32[]{:S(2)}, u32[]{:S(2)}) collective-permute-start(f32[3,8,8,128]{3,2,1,0:T(8,128)S(1)} %get-tuple-element.39), channel_id=1, source_target_pairs={{0,1},{2,3},{4,5},{6,7},{8,9},{10,11},{12,13},{14,15},{16,17},{18,... | collective-permute-start | bytes 294920 | tf_op jit(solution)/shard_map/ppermute | solution.py:16
  12.2 3.3 collective-permute-start.1
  15.7 8.2 %collective-permute-start.2 = (f32[3,8,2,128]{3,2,1,0:T(2,128)S(1)}, f32[3,8,2,128]{3,2,1,0:T(2,128)S(1)}, u32[]{:S(2)}, u32[]{:S(2)}) collective-permute-start(f32[3,8,2,128]{3,2,1,0:T(2,128)S(1)} %convolution_bitcast_fusion.2), channel_id=1, source_target_pairs={{0,2},{2,4},{4,6},{6,8},{8,10},{10,12},{12,14},{14,16},{16,18},{18... | collective-permute-start | bytes 73736 | tf_op jit(solution)/shard_map/ppermute | solution.py:16
  18.1 5.8 %collective-permute-start.3 = (f32[3,8,2,128]{3,2,1,0:T(2,128)S(1)}, f32[3,8,2,128]{3,2,1,0:T(2,128)S(1)}, u32[]{:S(2)}, u32[]{:S(2)}) collective-permute-start(f32[3,8,2,128]{3,2,1,0:T(2,128)S(1)} %convolution_bitcast_fusion.2), channel_id=1, source_target_pairs={{2,0},{4,2},{6,4},{8,6},{10,8},{12,10},{14,12},{16,14},{18,16},{20... | collective-permute-start | bytes 73736 | tf_op jit(solution)/shard_map/ppermute | solution.py:19
  154.5 1.1 copy-start.4
  255.8 2.3 copy-start.7
  257.0 1.1 copy-start.3
  319.4 6.2 %copy-start.8 = (f32[5,128,128]{1,2,0:T(8,128)}, f32[5,128,128]{1,2,0:T(8,128)S(1)}, u32[]{:S(2)}) copy-start(f32[5,128,128]{1,2,0:T(8,128)S(1)} %custom-call.39) | copy-start | bytes 983044
  334.7 2.7 copy-start.2
  337.5 1.6 copy-start.5
  337.5 1.6 copy-start.6
Sparse Core Ops, SparseCore 0:
  15.2 133.6 all-reduce.5
where the time goes:
time: 351 us; the launch traced here: 347 us
  other arithmetic  149 us (42%)
  waiting for transfers between devices  83.3 us (24%)
  blocking collectives  41.3 us (12%)
  local copies, waits for them, and re-layouts  22.5 us (6%)
  matrix products  22.2 us (6%)
  between operations  18.6 us (5%)
  starting transfers between devices  10.2 us (3%)
    another operation x16, other arithmetic, local(): lower = jnp.linalg.cholesky(gram)  89.1 us
    psum x1, waiting for transfers between devices, local(): lax.psum(jnp.einsum('rk,rj->kj', flat_rows, flat_rows, preferred_element_...  81.6 us
    another operation x8, other arithmetic, local(): lax.linalg.triangular_solve(lower, stack.astype(jnp.float32), left_side=F...  52 us
    psum x1, blocking collectives, local(): lax.psum((jnp.einsum('rk,r->k', flat_rows, filtered, preferred_element_ty...  41.3 us
    another operation x8, matrix products, local(): lax.linalg.triangular_solve(lower, stack.astype(jnp.float32), left_side=F...  13.5 us
    another operation x12, local copies, waits for them, and re-layouts  11.3 us
  transfers between devices with their start and end apart: 5, of which 2 were waited for; matrix products, arithmetic and copies ran while one was open for 1% of the time, Pallas kernels for 0%

commit v1 on v0

--- a/solution.py
+++ b/solution.py
@@ -36,9 +36,12 @@
     modes = basis.shape[-1]
     flat_rows = basis.reshape(-1, modes)
     total = flat_rows.shape[0] * lax.axis_size("gx") * lax.axis_size("gy")
-    mode_part = lax.psum(
-        jnp.einsum("rk,rj->kj", flat_rows, flat_rows, preferred_element_type=jnp.float32),
-        ("gx", "gy"),
+    mode_part = jnp.sum(
+        lax.all_gather(
+            jnp.einsum("rk,rj->kj", flat_rows, flat_rows, preferred_element_type=jnp.float32),
+            ("gx", "gy"),
+        ),
+        axis=0,
     )
     matrix_z = band(taps[2], cells_z, cells_z // STRIDE, STRIDE, True)
     along_z = jnp.dot(snapshot.reshape(-1, cells_z), matrix_z, preferred_element_type=jnp.float32)

time: 351 us -> 432 us (1.23)
  waiting for transfers between devices: 83.3 us -> 142 us
  other arithmetic: 149 us -> 162 us
  local copies, waits for them, and re-layouts: 22.5 us -> 27.9 us
    all_gather x0 -> x1, waiting for transfers between devices: none -> 138 us  [local(): lax.all_gather(jnp.einsum('rk,rj->kj', flat_rows, flat_rows, preferred_el...]
    psum x1 -> x0, waiting for transfers between devices: 81.6 us -> none  [local(): lax.psum(jnp.einsum('rk,rj->kj', flat_rows, flat_rows, preferred_element_...]
    reduce_sum x0 -> x1, other arithmetic: none -> 13.7 us  [local(): jnp.sum(lax.all_gather(jnp.einsum('rk,rj->kj', flat_rows, flat_rows, pref...]
  transfers between devices with their start and end apart: 5 -> 5, of which waited for: 2 -> 4; matrix products, arithmetic and copies ran while one was open for 1% -> 1% of each run, Pallas kernels for 0% -> 0%
where the time goes in v1:
time: 432 us; the launch traced here: 427 us
  other arithmetic  162 us (38%)
  waiting for transfers between devices  142 us (33%)
  blocking collectives  42.9 us (10%)
  local copies, waits for them, and re-layouts  27.9 us (6%)
  matrix products  23.6 us (5%)
  between operations  18.6 us (4%)
  starting transfers between devices  10.2 us (2%)
    all_gather x1, waiting for transfers between devices, local(): lax.all_gather(jnp.einsum('rk,rj->kj', flat_rows, flat_rows, preferred_el...  138 us
    another operation x16, other arithmetic, local(): lower = jnp.linalg.cholesky(gram)  89.1 us
    another operation x8, other arithmetic, local(): lax.linalg.triangular_solve(lower, stack.astype(jnp.float32), left_side=F...  52.9 us
    psum x1, blocking collectives, local(): lax.psum((jnp.einsum('rk,r->k', flat_rows, filtered, preferred_element_ty...  42.9 us
    another operation x12, local copies, waits for them, and re-layouts  14.2 us
    reduce_sum x1, other arithmetic, local(): jnp.sum(lax.all_gather(jnp.einsum('rk,rj->kj', flat_rows, flat_rows, pref...  13.7 us
    another operation x8, matrix products, local(): lax.linalg.triangular_solve(lower, stack.astype(jnp.float32), left_side=F...  13.5 us
  transfers between devices with their start and end apart: 5, of which 4 were waited for; matrix products, arithmetic and copies ran while one was open for 1% of the time, Pallas kernels for 0%

profile of v1, /device:TPU:0, one launch (start us, length us, event | category | flops | bytes accessed | tf_op | source)
XLA Modules:
  0.0 427.2 jit_solution(13529952083618031544)
XLA Ops:
  7.2 3.0 convolution_bitcast_fusion
  10.5 0.9 fusion.1
  12.0 2.4 collective-permute-start
  14.5 1.3 collective-permute-start.1
  16.1 1.5 collective-permute-done.1
  17.9 2.4 collective-permute-start.2
  20.3 4.1 collective-permute-start.3
  24.3 1.7 collective-permute-done.2
  26.3 0.6 multiply_reduce_fusion
  27.2 42.9 %all-reduce.3 = (f32[1]{0:T(128)}, f32[512]{0:T(512)S(1)}) all-reduce(f32[1]{0:T(128)} %bitcast.21, f32[512]{0:T(512)S(1)} %bitcast.155), channel_id=1, replica_groups=mesh['gx'=16,'gy'=2] {'gx','gy'}, use_global_device_ids=true, to_apply=%region_6.7 | all-reduce | flops 513 | bytes 4104 | tf_op jit(solution)/shard_map/psum | solution.py:58
  70.4 0.7 pad_maximum_fusion.4
  71.2 138.2 %all-gather.3.cloned.1.call-done = f32[16384,512]{1,0:T(8,128)} async-done(((f32[512,512]{1,0:T(8,128)}), f32[16384,512]{1,0:T(8,128)}) %all-gather.3.cloned.1.call-update) | async-done | bytes 33554448 | tf_op jit(solution)/shard_map/all_gather | solution.py:40
  209.4 13.7 %reduce_sum.54 = f32[512,512]{1,0:T(8,128)} reduce(f32[32,512,512]{2,1,0:T(8,128)} %bitcast.136, f32[]{:T(128)} %constant.182.clone.1), dimensions={0}, to_apply=%region_0.0 | reduce | flops 8126464 | bytes 34603012 | tf_op jit(solution)/shard_map/reduce_sum | solution.py:39
  223.1 1.6 copy.77
  224.7 1.2 maximum_multiply_fusion
  225.9 2.9 copy.79
  228.7 1.5 fusion.10
  230.3 1.1 copy-done.4
  231.3 11.7 %cholesky.131 = f32[128,128]{1,0:T(8,128)S(1)} custom-call(f32[128,128]{1,0:T(8,128)S(1)} %cholesky.333), custom_call_target="Cholesky" | custom-call | tf_op jit(solution)/shard_map/jit(cholesky)/cholesky | solution.py:69
  243.2 1.2 cholesky.348
  244.4 9.8 %custom-call.35 = f32[1,128,128]{1,2,0:T(8,128)S(1)} custom-call(f32[1,128,128]{2,1,0:T(8,128)S(1)} %get-tuple-element.54), custom_call_target="InvertDiagBlocksLowerTriangular" | custom-call | tf_op jit(solution)/shard_map/jit(cholesky)/cholesky | solution.py:69
  254.2 1.4 constant_dynamic-update-slice_fusion.2
  255.6 1.4 convolution_subtract_fusion.3
  257.0 11.7 %cholesky.264 = f32[128,128]{1,0:T(8,128)S(1)} custom-call(f32[128,128]{1,0:T(8,128)S(1)} %cholesky.337), custom_call_target="Cholesky" | custom-call | tf_op jit(solution)/shard_map/jit(cholesky)/cholesky | solution.py:69
  268.8 9.9 %custom-call.36 = f32[1,128,128]{1,2,0:T(8,128)S(1)} custom-call(f32[1,128,128]{2,1,0:T(8,128)S(1)} %get-tuple-element.51), custom_call_target="InvertDiagBlocksLowerTriangular" | custom-call | tf_op jit(solution)/shard_map/jit(cholesky)/cholesky | solution.py:69
  279.1 1.3 convolution_subtract_fusion.4
  280.4 11.7 %cholesky.285 = f32[128,128]{1,0:T(8,128)S(1)} custom-call(f32[128,128]{1,0:T(8,128)S(1)} %cholesky.342), custom_call_target="Cholesky" | custom-call | tf_op jit(solution)/shard_map/jit(cholesky)/cholesky | solution.py:69
  292.1 9.8 %custom-call.37 = f32[1,128,128]{1,2,0:T(8,128)S(1)} custom-call(f32[1,128,128]{2,1,0:T(8,128)S(1)} %get-tuple-element.48), custom_call_target="InvertDiagBlocksLowerTriangular" | custom-call | tf_op jit(solution)/shard_map/jit(cholesky)/cholesky | solution.py:69
  302.2 1.3 convolution_subtract_fusion.5
  303.5 11.9 %cholesky.304 = f32[128,128]{1,0:T(8,128)S(1)} custom-call(f32[128,128]{1,0:T(8,128)S(1)} %cholesky.347), custom_call_target="Cholesky" | custom-call | tf_op jit(solution)/shard_map/jit(cholesky)/cholesky | solution.py:69
  315.5 9.8 %custom-call.38 = f32[1,128,128]{1,2,0:T(8,128)S(1)} custom-call(f32[1,128,128]{2,1,0:T(8,128)S(1)} %get-tuple-element.45), custom_call_target="InvertDiagBlocksLowerTriangular" | custom-call | tf_op jit(solution)/shard_map/jit(cholesky)/cholesky | solution.py:69
  325.6 0.6 multiply_reduce_fusion.1
  327.6 0.7 compare_reduce_fusion.1
  328.3 0.6 compare_reduce_fusion
  329.0 0.6 compare_reduce_fusion.2
  332.1 1.2 fusion.20
  333.4 0.5 triangular_solve.195
  333.9 0.5 copy-done.3
  334.5 14.2 %while.1 = (s32[]{:T(128)}, f32[513,513]{1,0:T(8,128)}, s32[4,2]{0,1:T(2,128)S(1)}, f32[4,128,128]{2,1,0:T(8,128)}, s32[]{:T(128)}) while((s32[]{:T(128)}, f32[513,513]{1,0:T(8,128)}, s32[4,2]{0,1:T(2,128)S(1)}, f32[4,128,128]{2,1,0:T(8,128)}, s32[]{:T(128)}) %tuple.51), condition=%wide.while_cond, body=%wide.while_body.sunk | while | flops 2 | bytes 132705 | solution.py:70
  334.5 0.6 fusion.83
  335.1 2.9 bitcast_dynamic-update-slice_fusion.2
  338.1 0.6 fusion.83
  338.7 2.9 bitcast_dynamic-update-slice_fusion.2
  341.6 0.6 fusion.83
  342.2 2.9 bitcast_dynamic-update-slice_fusion.2
  345.2 0.6 fusion.83
  345.8 2.9 bitcast_dynamic-update-slice_fusion.2
  348.6 0.7 fusion.53
  349.4 1.0 pad_maximum_fusion.1
  350.3 49.1 %custom-call.39 = f32[5,128,128]{1,2,0:T(8,128)S(1)} custom-call(f32[5,128,128]{2,1,0:T(8,128)S(1)} %pad_maximum_fusion.1), custom_call_target="InvertDiagBlocksLowerTriangular" | custom-call | tf_op jit(solution)/shard_map/triangular_solve | solution.py:70
  399.5 0.6 triangular_solve.205
  400.1 1.1 bitcast_convert_fusion
  401.1 1.6 convolution_subtract_fusion.1
  403.4 2.3 convolution_subtract_fusion.2
  405.7 1.1 fusion.73
  407.0 3.0 convolution_subtract_fusion
  410.0 2.0 fusion.72
  412.0 0.9 copy.90
  412.9 1.9 fusion.17
  414.9 1.0 fusion.34
  415.9 0.6 triangular_solve.193
  416.5 1.1 copy.104
  417.6 1.5 copy.93
  419.2 1.0 pad_maximum_fusion
  (63 shorter events, 4.7 us)
Async XLA Ops:
  7.2 4.3 %copy-start = (bf16[3,8,16,1024]{3,2,1,0:T(8,128)(2,1)S(1)}, bf16[3,8,16,1024]{3,2,1,0:T(8,128)(2,1)}, u32[]{:S(2)}) copy-start(bf16[3,8,16,1024]{3,2,1,0:T(8,128)(2,1)} %param.3) | copy-start | bytes 2359300
  7.2 3.1 copy-start.8
  7.2 202.2 %all-gather.3.cloned.1.call-start = ((), (), s32[]{:S(2)}) async-start(), calls=%async_computation | async-start | bytes 34603008 | tf_op jit(solution)/shard_map/all_gather | solution.py:40
  11.5 15.5 %copy-start.1 = (bf16[3,1,2,128,512]{4,3,2,1,0:T(8,128)(2,1)S(1)}, bf16[3,1,2,128,512]{4,3,2,1,0:T(8,128)(2,1)}, u32[]{:S(2)}) copy-start(bf16[3,1,2,128,512]{4,3,2,1,0:T(8,128)(2,1)} %param.4) | copy-start | bytes 2359300
  12.0 4.1 collective-permute-start
  14.5 3.2 collective-permute-start.1
  17.9 8.2 %collective-permute-start.2 = (f32[3,8,2,128]{3,2,1,0:T(2,128)S(1)}, f32[3,8,2,128]{3,2,1,0:T(2,128)S(1)}, u32[]{:S(2)}, u32[]{:S(2)}) collective-permute-start(f32[3,8,2,128]{3,2,1,0:T(2,128)S(1)} %convolution_bitcast_fusion.2), channel_id=1, source_target_pairs={{0,2},{2,4},{4,6},{6,8},{8,10},{10,12},{12,14},{14,16},{16,18},{18... | collective-permute-start | bytes 73736 | tf_op jit(solution)/shard_map/ppermute | solution.py:16
  20.3 5.9 %collective-permute-start.3 = (f32[3,8,2,128]{3,2,1,0:T(2,128)S(1)}, f32[3,8,2,128]{3,2,1,0:T(2,128)S(1)}, u32[]{:S(2)}, u32[]{:S(2)}) collective-permute-start(f32[3,8,2,128]{3,2,1,0:T(2,128)S(1)} %convolution_bitcast_fusion.2), channel_id=1, source_target_pairs={{2,0},{4,2},{6,4},{8,6},{10,8},{12,10},{14,12},{16,14},{18,16},{20... | collective-permute-start | bytes 73736 | tf_op jit(solution)/shard_map/ppermute | solution.py:19
  230.3 1.1 copy-start.4
  333.4 1.1 copy-start.3
  399.5 6.2 %copy-start.7 = (f32[5,128,128]{1,2,0:T(8,128)}, f32[5,128,128]{1,2,0:T(8,128)S(1)}, u32[]{:S(2)}) copy-start(f32[5,128,128]{1,2,0:T(8,128)S(1)} %custom-call.39) | copy-start | bytes 983044
  414.9 2.7 copy-start.2
  417.6 1.6 copy-start.5
  417.6 1.6 copy-start.6
Sparse Core Ops, SparseCore 0:
  11.4 197.9 all-gather.2
